TPU v7x, 32 devices: a whole 2x2x4 slice. The times are simulated.
32 devices in a mesh: row: 4 (over y, x), col: 8 (over z, core).
Axes of the slice: x: 2, y: 2, z: 4, core: 2. Of those that a mesh axis runs over, the one named last changes fastest.
Arguments:
- tokens: bfloat16 [512, 16384], P('col', 'row'), may hold values from -6 to 6
- weight: bfloat16 [16384, 32768], P('row', 'col'), may hold values from -0.21875 to 0.21875
- logits: float32 [3, 32768], P(None, 'col'), may hold values from -6 to 303
- cotangent: bfloat16 [512, 32768], P('row', 'col'), may hold values from -6 to 6
Outputs:
- mixed_out: bfloat16 [512, 32768], P('row', 'col')
- input_grad: bfloat16 [512, 16384], P('col', 'row')
- weight_grad: bfloat16 [16384, 32768], P('row', 'col')
- logit_grad: float32 [3, 32768], P(None, 'col')
All inputs are finite; a program needn't handle non-finite values.
Results may differ from a plain program's by a relative error of at most 0.0049.
Values may be sent and summed in bfloat16 or wider, within the bound.
No kernel may reach another device: no remote copies, remote signals or barrier semaphores. Data moves between devices by JAX's collectives and lax.ppermute only.
A program may use at most 192 MiB of HBM per device.

v0:
```python
import math
import jax
import jax.numpy as jnp
from jax import lax
from jax.sharding import PartitionSpec as P

EPSILON = 1e-06
TWO_PI = 2.0 * math.pi
grid_levels = (1.0, 7.0, 127.0)


def quantize(master, peak, scores):
    shares = jax.nn.softmax(scores, axis=0)
    blended = jnp.zeros_like(master)
    slopes = jnp.zeros_like(master)
    candidates = []
    for number, level_value in enumerate(grid_levels):
        spacing = (peak + EPSILON) / level_value
        scaled = master / spacing
        angle_value = TWO_PI * scaled
        candidate = spacing * (scaled - jnp.sin(angle_value) / TWO_PI)
        blended = blended + shares[number] * candidate
        slopes = slopes + shares[number] * (1.0 - jnp.cos(angle_value))
        candidates.append(candidate)
    return (shares, blended, slopes, candidates)


def logit_slopes(shares, terms):
    return shares * (terms - jnp.sum(shares * terms, axis=0, keepdims=True))


def shards(tokens, weight, logits, cotangent):
    master = weight.astype(jnp.float32)
    peak = lax.pmax(jnp.max(jnp.abs(master), axis=0), "row")
    shares, blended, slopes, candidates = quantize(master, peak, logits)
    blend_half = blended.astype(jnp.bfloat16)
    all_cotangent = lax.all_gather(cotangent, "row", axis=0, tiled=True)
    shard_piece = lax.all_gather(tokens, "col", axis=0, tiled=True)
    product = jnp.dot(shard_piece, blend_half, preferred_element_type=jnp.float32)
    outputs_part = product
    outputs_part, all_tokens = (outputs_part, shard_piece)
    mixed_grad = lax.dot_general(
        all_tokens, all_cotangent, (((0,), (0,)), ((), ())), preferred_element_type=jnp.float32
    )
    out_rows = cotangent.shape[0]
    in_rows = tokens.shape[0]
    summed_output = lax.psum(outputs_part, "row")
    outputs_mine = lax.dynamic_slice_in_dim(
        summed_output, lax.axis_index("row") * out_rows, out_rows, 0
    )
    summed_input = lax.psum(
        lax.dot_general(
            all_cotangent, blend_half, (((1,), (1,)), ((), ())), preferred_element_type=jnp.float32
        ),
        "col",
    )
    input_mine = lax.dynamic_slice_in_dim(summed_input, lax.axis_index("col") * in_rows, in_rows, 0)
    mixed_out = outputs_mine.astype(jnp.bfloat16)
    input_grad = input_mine.astype(jnp.bfloat16)
    weight_grad = (mixed_grad * slopes).astype(jnp.bfloat16)
    local_terms = jnp.stack([jnp.sum(mixed_grad * candidate, axis=0) for candidate in candidates])
    terms = lax.psum(local_terms, "row")
    logit_grad = logit_slopes(shares, terms)
    return (mixed_out, input_grad, weight_grad, logit_grad)


def solution(mesh):
    in_specs = (P("col", "row"), P("row", "col"), P(None, "col"), P("row", "col"))
    out_specs = (P("row", "col"), P("col", "row"), P("row", "col"), P(None, "col"))
    return jax.shard_map(shards, mesh=mesh, in_specs=in_specs, out_specs=out_specs, check_vma=False)
```

profile of v0, /device:TPU:0, one launch (start us, length us, event | category | flops | bytes accessed | tf_op | source)
XLA Modules:
  0.0 1547.8 jit_solution(15201740005334068569)
XLA Ops:
  7.2 0.0 copy-start
  7.2 0.0 all-gather.5.cloned.1.call-start
  7.2 0.7 all-gather.5.cloned.1.call-update
  7.9 0.0 all-gather.3.cloned.1.call-start
  8.0 0.7 all-gather.3.cloned.1.call-update
  8.7 0.9 reduce_max.18
  9.6 0.0 copy-start.2
  9.6 11.9 fusion
  21.5 18.4 %pmax.7 = f32[4096]{0:T(1024)S(1)} all-reduce(f32[4096]{0:T(1024)S(1)} %fusion), channel_id=1, replica_groups=mesh['row'=4,'col'=8] {'row'}, use_global_device_ids=true, to_apply=%region_3.0 | all-reduce | flops 4096 | bytes 32768 | tf_op jit(solution)/shard_map/pmax | solution.py:34
  39.9 0.0 copy-done
  39.9 0.1 fusion.2
  39.9 0.0 copy-start.4
  40.0 0.5 copy-done.4
  40.6 24.7 %all-gather.5.cloned.1.call-done = bf16[512,4096]{1,0:T(8,128)(2,1)} async-done(((bf16[128,4096]{1,0:T(8,128)(2,1)}), bf16[512,4096]{1,0:T(8,128)(2,1)}) %all-gather.5.cloned.1.call-update) | async-done | bytes 4194320 | tf_op jit(solution)/shard_map/all_gather | solution.py:37
  65.3 48.5 %all-gather.3.cloned.1.call-done = bf16[512,4096]{1,0:T(8,128)(2,1)} async-done(((bf16[64,4096]{1,0:T(8,128)(2,1)}), bf16[512,4096]{1,0:T(8,128)(2,1)}) %all-gather.3.cloned.1.call-update) | async-done | bytes 4194320 | tf_op jit(solution)/shard_map/all_gather | solution.py:38
  113.8 0.0 copy-start.6
  113.8 917.4 %multiply_reduce_fusion.2 = (f32[4096]{0:T(1024)S(1)}, f32[4096]{0:T(1024)S(1)}, f32[4096]{0:T(1024)S(1)}, bf16[4096,4096]{1,0:T(8,128)(2,1)}, bf16[4096,4096]{1,0:T(8,128)(2,1)}) fusion(f32[4096]{0:T(1024)S(1)} %get-tuple-element.18, bf16[4096,4096]{1,0:T(8,128)(2,1)} %param.5, f32[4096]{0:T(1024)S(1)} %get-tuple-element.20, ...), kind=kOutput, calls=%fused_computation.7 | convolution fusion | flops 17817391104 | bytes 109199360 | tf_op jit(solution)/shard_map/dot_general | solution.py:42
  1031.2 0.0 copy-done.2
  1031.2 0.0 copy-done.6
  1031.2 24.5 %convolution_bitcast_fusion.1 = f32[512,4096]{0,1:T(8,128)} fusion(bf16[4096,4096]{1,0:T(8,128)(2,1)} %get-tuple-element.14, bf16[512,4096]{1,0:T(8,128)(2,1)S(1)} %copy-done.6), kind=kOutput, calls=%fused_computation.14 | convolution fusion | flops 17179869184 | bytes 46137344 | tf_op jit(solution)/shard_map/dot_general | solution.py:39
  1055.8 286.1 %all-reduce.3 = (bf16[512,4096]{0,1:T(8,128)(2,1)}, f32[3,4096]{1,0:T(4,128)S(1)}) all-reduce(f32[512,4096]{0,1:T(8,128)} %convolution_bitcast_fusion.1, f32[3,4096]{1,0:T(4,128)S(1)} %pad_maximum_fusion), channel_id=1, replica_groups=mesh['row'=4,'col'=8] {'row'}, use_global_device_ids=true, to_apply=%region_4.0 | all-reduce | flops 2109440 | bytes 12681216 | tf_op jit(solution)/shard_map/psum | solution.py:47
  1342.0 1.3 dynamic-slice_convert_fusion.1
  1343.3 1.3 copy.8
  1344.6 25.0 %convolution_bitcast_fusion = f32[512,4096]{0,1:T(8,128)} fusion(bf16[4096,4096]{1,0:T(8,128)(2,1)} %get-tuple-element.14, bf16[512,4096]{1,0:T(8,128)(2,1)} %all-gather.5.cloned.1.call-done), kind=kOutput, calls=%fused_computation.13 | convolution fusion | flops 17179869184 | bytes 46137344 | tf_op jit(solution)/shard_map/dot_general | solution.py:52
  1369.6 167.9 %all-reduce.4 = bf16[512,4096]{0,1:T(8,128)(2,1)} all-reduce(f32[512,4096]{0,1:T(8,128)} %convolution_bitcast_fusion), channel_id=1, replica_groups=mesh['row'=4,'col'=8] {'col'}, use_global_device_ids=true, to_apply=%region_5.0 | all-reduce | flops 2097152 | bytes 12582912 | tf_op jit(solution)/shard_map/psum | solution.py:51
  1537.5 1.6 dynamic-slice_convert_fusion
  1539.1 1.1 copy.9
  1540.2 0.0 copy-done.1
  1540.2 0.0 copy-done.3
  1540.2 0.0 copy-done.5
  1540.2 0.1 multiply_reduce_fusion.3
  1540.3 0.7 subtract_multiply_fusion.3
  (7 shorter events, 0.1 us)
Async XLA Ops:
  7.2 32.7 %copy-start = (f32[3,4096]{1,0:T(4,128)S(1)}, f32[3,4096]{1,0:T(4,128)}, u32[]{:S(2)}) copy-start(f32[3,4096]{1,0:T(4,128)} %param.6) | copy-start | bytes 147460
  7.2 58.1 %all-gather.5.cloned.1.call-start = ((), (), s32[]{:S(2)}) async-start(), calls=%async_computation.1 | async-start | bytes 5242880 | tf_op jit(solution)/shard_map/all_gather | solution.py:37
  7.9 105.9 %all-gather.3.cloned.1.call-start = ((), (), s32[]{:S(2)}) async-start(), calls=%async_computation | async-start | bytes 4718592 | tf_op jit(solution)/shard_map/all_gather | solution.py:38
  9.6 1021.7 %copy-start.2 = (f32[4096]{0:T(1024)}, f32[4096]{0:T(1024)S(1)}, u32[]{:S(2)}) copy-start(f32[4096]{0:T(1024)S(1)} %reduce_max.18) | copy-start | bytes 49156
  39.9 0.6 copy-start.4
  113.8 917.5 %copy-start.6 = (bf16[512,4096]{1,0:T(8,128)(2,1)S(1)}, bf16[512,4096]{1,0:T(8,128)(2,1)}, u32[]{:S(2)}) copy-start(bf16[512,4096]{1,0:T(8,128)(2,1)} %all-gather.3.cloned.1.call-done) | copy-start | bytes 12582916
  1344.6 195.7 %copy-start.1 = (f32[3,4096]{1,0:T(4,128)S(1)}, f32[3,4096]{1,0:T(4,128)}, u32[]{:S(2)}) copy-start(f32[3,4096]{1,0:T(4,128)} %param.6) | copy-start | bytes 147460
  1344.6 195.7 %copy-start.3 = (f32[4096]{0:T(1024)S(1)}, f32[4096]{0:T(1024)}, u32[]{:S(2)}) copy-start(f32[4096]{0:T(1024)} %copy-done.2) | copy-start | bytes 49156
  1344.6 195.7 %copy-start.5 = (f32[4096]{0:T(1024)S(1)}, f32[4096]{0:T(1024)}, u32[]{:S(2)}) copy-start(f32[4096]{0:T(1024)} %copy-done.4) | copy-start | bytes 49156
Sparse Core Ops, SparseCore 0:
  9.8 55.4 all-gather.4
  66.9 46.8 all-gather.2
where the time goes:
time: 1550 us
  matrix products  967 us (62%)
  blocking collectives  472 us (30%)
  waiting for transfers between devices  74.6 us (5%)
    dot_general x1, matrix products, shards(): lax.dot_general(all_tokens, all_cotangent, (((0,), (0,)), ((), ())), pref...  917 us
    psum x1, blocking collectives, shards(): summed_output = lax.psum(outputs_part, 'row')  286 us
    psum x1, blocking collectives, shards(): lax.psum(lax.dot_general(all_cotangent, blend_half, (((1,), (1,)), ((), (...  168 us
    all_gather x1, waiting for transfers between devices, shards(): shard_piece = lax.all_gather(tokens, 'col', axis=0, tiled=True)  48.5 us
  transfers between devices with their start and end apart: 2, of which 2 were waited for; matrix products, arithmetic and copies ran while one was open for 1% of the time, Pallas kernels for 0%

commit v1 on v0

--- a/solution.py
+++ b/solution.py
@@ -44,7 +44,16 @@
     )
     out_rows = cotangent.shape[0]
     in_rows = tokens.shape[0]
-    summed_output = lax.psum(outputs_part, "row")
+
+    def advance_domain(tile_in):
+        total_devices = lax.axis_size("row")
+        plain = lambda part_next: [(s, s ^ part_next) for s in range(total_devices)]
+        wide_out = tile_in
+        for j0 in range(total_devices.bit_length() - 1):
+            wide_out = wide_out + lax.ppermute(wide_out, axis_name="row", perm=plain(1 << j0))
+        return wide_out
+
+    summed_output = advance_domain(outputs_part)
     outputs_mine = lax.dynamic_slice_in_dim(
         summed_output, lax.axis_index("row") * out_rows, out_rows, 0
     )

time: 1550 us -> 2140 us (1.38)
  other arithmetic: 13.7 us -> 790 us
  blocking collectives: 472 us -> 203 us
  waiting for transfers between devices: 74.6 us -> 234 us
  matrix products: 967 us -> 880 us
    convert_element_type x0 -> x2, other arithmetic: none -> 764 us  [the longest x1 761 us: shards(): weight_grad = (mixed_grad * slopes).astype(jnp.bfloat16)]
    psum x1, blocking collectives: 286 us -> 16.9 us  [shards(): terms = lax.psum(local_terms, 'row')]
    ppermute x0 -> x2, waiting for transfers between devices: none -> 160 us  [advance_domain(): lax.ppermute(wide_out, axis_name='row', perm=plain(1 << j0))]
    dot_general x1, matrix products: 917 us -> 830 us  [shards(): lax.dot_general(all_tokens, all_cotangent, (((0,), (0,)), ((), ())), pref...]
  transfers between devices with their start and end apart: 2 -> 4, of which waited for: 2 -> 4; matrix products, arithmetic and copies ran while one was open for 1% -> 2% of each run, Pallas kernels for 0% -> 0%
where the time goes in v1:
time: 2140 us; the launch traced here: 2130 us
  matrix products  880 us (41%)
  other arithmetic  790 us (37%)
  waiting for transfers between devices  234 us (11%)
  blocking collectives  203 us (9%)
    dot_general x1, matrix products, shards(): lax.dot_general(all_tokens, all_cotangent, (((0,), (0,)), ((), ())), pref...  830 us
    convert_element_type x1, other arithmetic, shards(): weight_grad = (mixed_grad * slopes).astype(jnp.bfloat16)  761 us
    psum x1, blocking collectives, shards(): lax.psum(lax.dot_general(all_cotangent, blend_half, (((1,), (1,)), ((), (...  168 us
    ppermute x2, waiting for transfers between devices, advance_domain(): lax.ppermute(wide_out, axis_name='row', perm=plain(1 << j0))  160 us
    all_gather x1, waiting for transfers between devices, shards(): shard_piece = lax.all_gather(tokens, 'col', axis=0, tiled=True)  48.5 us
  transfers between devices with their start and end apart: 4, of which 4 were waited for; matrix products, arithmetic and copies ran while one was open for 2% of the time, Pallas kernels for 0%

profile of v1, /device:TPU:0, one launch (start us, length us, event | category | flops | bytes accessed | tf_op | source)
XLA Modules:
  0.0 2126.3 jit_solution(13486704479878830599)
XLA Ops:
  7.2 0.0 all-gather.5.cloned.1.call-start
  7.2 0.7 all-gather.5.cloned.1.call-update
  7.9 0.0 all-gather.3.cloned.1.call-start
  7.9 0.7 all-gather.3.cloned.1.call-update
  8.6 0.9 reduce_max.18
  9.5 0.0 copy-start.1
  9.5 11.9 fusion
  21.5 18.4 pmax.7
  39.8 1.5 fusion.3
  41.4 23.9 %all-gather.5.cloned.1.call-done = bf16[512,4096]{1,0:T(8,128)(2,1)} async-done(((bf16[128,4096]{1,0:T(8,128)(2,1)}), bf16[512,4096]{1,0:T(8,128)(2,1)}) %all-gather.5.cloned.1.call-update) | async-done | bytes 4194320 | tf_op jit(solution)/shard_map/all_gather | solution.py:37
  65.3 48.5 %all-gather.3.cloned.1.call-done = bf16[512,4096]{1,0:T(8,128)(2,1)} async-done(((bf16[64,4096]{1,0:T(8,128)(2,1)}), bf16[512,4096]{1,0:T(8,128)(2,1)}) %all-gather.3.cloned.1.call-update) | async-done | bytes 4194320 | tf_op jit(solution)/shard_map/all_gather | solution.py:38
  113.8 0.0 copy-done.1
  113.8 830.3 %multiply_reduce_fusion.2 = (f32[4096]{0:T(1024)S(1)}, f32[4096]{0:T(1024)S(1)}, f32[4096]{0:T(1024)S(1)}, f32[4096,4096]{1,0:T(8,128)}) fusion(f32[4096]{0:T(1024)S(1)} %get-tuple-element.20, bf16[4096,4096]{1,0:T(8,128)(2,1)} %param.5, f32[4096]{0:T(1024)S(1)} %get-tuple-element.19, f32[4096]{0:T(1024)S(1)} %get-tuple-element.18, ...), kind=kOutput, calls=%fused_computation.7 | convolution fusion | flops 17548955648 | bytes 109150208 | tf_op jit(solution)/shard_map/dot_general | solution.py:42
  944.1 16.9 psum.15
  961.0 0.0 copy-done
  961.0 0.0 copy-done.2
  961.0 0.1 multiply_reduce_fusion.3
  961.2 761.1 %multiply_convert_fusion = (bf16[4096,4096]{1,0:T(8,128)(2,1)}, bf16[4096,4096]{1,0:T(8,128)(2,1)}) fusion(f32[4096,4096]{1,0:T(8,128)} %get-tuple-element.21, f32[4096]{0:T(1024)S(1)} %bitcast.20, f32[4096]{0:T(1024)S(1)} %bitcast.21, f32[4096]{0:T(1024)S(1)} %bitcast.19, f32[4096]{0:T(1024)S(1)} %get-tuple-element.20, bf16[4096,4096]{1,0:T(8,128)(2,1)} %param.5, ...), kind=kLoop, calls=%fused_computation.8 | loop fusion | flops 536870912 | bytes 167870464 | tf_op jit(solution)/shard_map/convert_element_type | solution.py:69
  1722.3 0.0 copy-done.4
  1722.3 24.4 %convolution_bitcast_fusion.1 = f32[512,4096]{0,1:T(8,128)} fusion(bf16[4096,4096]{1,0:T(8,128)(2,1)} %get-tuple-element.14, bf16[512,4096]{1,0:T(8,128)(2,1)S(1)} %copy-done.4), kind=kOutput, calls=%fused_computation.14 | convolution fusion | flops 17179869184 | bytes 46137344 | tf_op jit(solution)/shard_map/dot_general | solution.py:39
  1746.7 0.0 collective-permute-start
  1746.7 25.2 %convolution_bitcast_fusion = f32[512,4096]{0,1:T(8,128)} fusion(bf16[4096,4096]{1,0:T(8,128)(2,1)} %get-tuple-element.14, bf16[512,4096]{1,0:T(8,128)(2,1)} %all-gather.5.cloned.1.call-done), kind=kOutput, calls=%fused_computation.13 | convolution fusion | flops 17179869184 | bytes 46137344 | tf_op jit(solution)/shard_map/dot_general | solution.py:61
  1771.9 153.9 %collective-permute-done = f32[512,4096]{0,1:T(8,128)} collective-permute-done((f32[512,4096]{0,1:T(8,128)}, f32[512,4096]{0,1:T(8,128)}, u32[]{:S(2)}, u32[]{:S(2)}) %collective-permute-start) | collective-permute-done | bytes 8388640 | tf_op jit(solution)/shard_map/ppermute | solution.py:53
  1925.8 11.1 add.36
  1936.9 0.6 collective-permute-start.1
  1937.6 167.9 %all-reduce.1 = bf16[512,4096]{0,1:T(8,128)(2,1)} all-reduce(f32[512,4096]{0,1:T(8,128)} %convolution_bitcast_fusion), channel_id=1, replica_groups=mesh['row'=4,'col'=8] {'col'}, use_global_device_ids=true, to_apply=%region_4.0 | all-reduce | flops 2097152 | bytes 12582912 | tf_op jit(solution)/shard_map/psum | solution.py:60
  2105.5 1.6 dynamic-slice_convert_fusion
  2107.1 1.1 copy.9
  2108.2 0.7 subtract_multiply_fusion.3
  2108.8 6.4 collective-permute-done.1
  2115.2 2.4 fusion.1
  2117.7 1.3 copy.8
  (8 shorter events, 0.1 us)
Async XLA Ops:
  7.2 58.1 %all-gather.5.cloned.1.call-start = ((), (), s32[]{:S(2)}) async-start(), calls=%async_computation.1 | async-start | bytes 5242880 | tf_op jit(solution)/shard_map/all_gather | solution.py:37
  7.9 105.9 %all-gather.3.cloned.1.call-start = ((), (), s32[]{:S(2)}) async-start(), calls=%async_computation | async-start | bytes 4718592 | tf_op jit(solution)/shard_map/all_gather | solution.py:38
  9.5 104.2 %copy-start.1 = (f32[4096]{0:T(1024)}, f32[4096]{0:T(1024)S(1)}, u32[]{:S(2)}) copy-start(f32[4096]{0:T(1024)S(1)} %reduce_max.18) | copy-start | bytes 49156
  113.8 847.2 %copy-start = (f32[3,4096]{1,0:T(4,128)S(1)}, f32[3,4096]{1,0:T(4,128)}, u32[]{:S(2)}) copy-start(f32[3,4096]{1,0:T(4,128)} %param.6) | copy-start | bytes 147460
  113.8 847.2 %copy-start.2 = (f32[4096]{0:T(1024)S(1)}, f32[4096]{0:T(1024)}, u32[]{:S(2)}) copy-start(f32[4096]{0:T(1024)} %copy-done.1) | copy-start | bytes 49156
  113.8 847.3 %copy-start.3 = (f32[4096]{0:T(1024)S(1)}, f32[4096]{0:T(1024)}, u32[]{:S(2)}) copy-start(f32[4096]{0:T(1024)} %fusion.3) | copy-start | bytes 49156
  961.2 761.1 %copy-start.4 = (bf16[512,4096]{1,0:T(8,128)(2,1)S(1)}, bf16[512,4096]{1,0:T(8,128)(2,1)}, u32[]{:S(2)}) copy-start(bf16[512,4096]{1,0:T(8,128)(2,1)} %all-gather.3.cloned.1.call-done) | copy-start | bytes 12582916
  1746.7 179.2 %collective-permute-start = (f32[512,4096]{0,1:T(8,128)}, f32[512,4096]{0,1:T(8,128)}, u32[]{:S(2)}, u32[]{:S(2)}) collective-permute-start(f32[512,4096]{0,1:T(8,128)} %convolution_bitcast_fusion.1), channel_id=1, source_target_pairs={{0,8},{8,0},{16,24},{24,16},{1,9},{9,1},{17,25},{25,17},{2,10},{10... | collective-permute-start | bytes 25165832 | tf_op jit(solution)/shard_map/ppermute | solution.py:53
  1936.9 178.3 %collective-permute-start.1 = (f32[512,4096]{0,1:T(8,128)}, f32[512,4096]{0,1:T(8,128)}, u32[]{:S(2)}, u32[]{:S(2)}) collective-permute-start(f32[512,4096]{0,1:T(8,128)} %add.36), channel_id=1, source_target_pairs={{0,16},{8,24},{16,0},{24,8},{1,17},{9,25},{17,1},{25,9},{2,18},{10... | collective-permute-start | bytes 25165832 | tf_op jit(solution)/shard_map/ppermute | solution.py:53
Sparse Core Ops, SparseCore 0:
  9.8 55.4 all-gather.4
  66.9 46.8 all-gather.2
